TPU v7x, 32 devices: a whole 2x2x4 slice. The times are simulated.
32 devices in a mesh: rep: 2 (over x), zero: 16 (over z, y, core).
Axes of the slice: x: 2, y: 2, z: 4, core: 2. Of those that a mesh axis runs over, the one named last changes fastest.
Arguments:
- gated_input: bfloat16 [2, 2048, 4096], P('rep', 'zero'), may hold values from -6 to 6
- query_gate: bfloat16 [2, 2048, 4096], P('rep', 'zero'), may hold values from -12 to 12
- cotangent: bfloat16 [2, 2048, 4096], P('rep', 'zero'), may hold values from -8 to 8
- filters: float32 [2, 256, 128], P('rep', 'zero'), may hold values from -0.5 to 0.5
- first_moment: float32 [2, 256, 128], P('rep', 'zero'), may hold values from -0.03125 to 0.03125
- second_moment: float32 [2, 256, 128], P('rep', 'zero'), may hold values from 1e-06 to 0.0001
- step_index: int32 [1], replicated, may hold values from 0 to 999
Outputs:
- query_grad: bfloat16 [2, 2048, 4096], P('rep', 'zero')
- input_grad: bfloat16 [2, 2048, 4096], P('rep', 'zero')
- new_filters: float32 [2, 256, 128], P('rep', 'zero')
All inputs are finite; a program needn't handle non-finite values.
Results may differ from a plain program's by a relative error of at most 0.007.
Values may be sent and summed in bfloat16 or wider, within the bound.
No kernel may reach another device: no remote copies, remote signals or barrier semaphores. Data moves between devices by JAX's collectives and lax.ppermute only.
A program may use at most 256 MiB of HBM per device.

v0:
```python
from functools import partial
import jax
import jax.numpy as jnp
from jax import lax
from jax.sharding import PartitionSpec as P

CLIP_NORM = 1.0
BETA_ONE = 0.9
BETA_TWO = 0.95
LEARN_RATE = 0.05
ADAM_EPS = 1e-08


def swapped(value, axis, apart):
    mask = 2**apart
    pairs = [(source, source ^ mask) for source in range(lax.axis_size(axis))]
    return lax.ppermute(value, axis, pairs)


def passed_along(block, axis, distance):
    devices = range(lax.axis_size(axis))
    route = [(i - distance, i) for i in devices if i - distance in devices]
    return lax.ppermute(block, axis, route)


def circulant(half_filters):
    groups_all, filter_len = half_filters.shape
    flipped = half_filters[:, ::-1]
    doubled = jnp.concatenate([flipped, flipped], axis=1)
    tiled = jnp.tile(doubled, (1, filter_len))
    trimmed = tiled[:, : filter_len * (2 * filter_len - 1)]
    return trimmed.reshape(groups_all, filter_len, 2 * filter_len - 1)[:, :, filter_len - 1 :]


def blocked(rows_major, groups_all, filter_len):
    tok_rows, channels = rows_major.shape
    return rows_major.T.reshape(
        groups_all, channels // groups_all, tok_rows // filter_len, filter_len
    )


def unblocked(blocks):
    groups_all, group_width, block_count, filter_len = blocks.shape
    return blocks.reshape(groups_all * group_width, block_count * filter_len).T


def swap_bit(values, bit_number):
    return swapped(values, "rep", bit_number)


def on_device(gated_input, query_gate, cotangent, filters, first_moment, second_moment, step_index):
    inputs = gated_input[0]
    gate_values = query_gate[0]
    upstream = cotangent[0]
    tok_rows, channels = inputs.shape
    filter_len = filters.shape[2]
    shard_len = filters.shape[1]
    half_filters = lax.all_gather(filters[0].astype(jnp.bfloat16), "zero", axis=0, tiled=True)
    groups_all = half_filters.shape[0]
    circ_table = circulant(half_filters)
    index_row = lax.broadcasted_iota(jnp.int32, (filter_len, filter_len), 0)
    index_col = lax.broadcasted_iota(jnp.int32, (filter_len, filter_len), 1)
    lower_mask = (index_row >= index_col)[None]
    zero_half = jnp.zeros((), jnp.bfloat16)
    table_cur = jnp.where(lower_mask, circ_table, zero_half)
    table_prev = jnp.where(lower_mask, zero_half, circ_table)
    upstream_wide = upstream.astype(jnp.float32)
    mixed_rows = (upstream_wide * gate_values.astype(jnp.float32)).astype(jnp.bfloat16)
    tail_rows = passed_along(inputs, "zero", 1)
    head_rows = passed_along(mixed_rows, "zero", -1)
    input_ext = jnp.concatenate([tail_rows, inputs], axis=0)
    mixed_ext = jnp.concatenate([mixed_rows, head_rows], axis=0)
    input_blocks = blocked(input_ext, groups_all, filter_len)
    mixed_blocks = blocked(mixed_ext, groups_all, filter_len)
    input_cur = input_blocks[:, :, 1:]
    input_prev = input_blocks[:, :, :-1]
    mixed_own = mixed_blocks[:, :, :-1]
    mixed_next = mixed_blocks[:, :, 1:]
    conv_out = jnp.einsum(
        "gik,gcbk->gcbi", table_cur, input_cur, preferred_element_type=jnp.float32
    )
    conv_out = conv_out + jnp.einsum(
        "gik,gcbk->gcbi", table_prev, input_prev, preferred_element_type=jnp.float32
    )
    query_grad = (upstream_wide * unblocked(conv_out)).astype(jnp.bfloat16)
    back_blocks = jnp.einsum(
        "gki,gcbk->gcbi", table_cur, mixed_own, preferred_element_type=jnp.float32
    )
    back_blocks = back_blocks + jnp.einsum(
        "gki,gcbk->gcbi", table_prev, mixed_next, preferred_element_type=jnp.float32
    )
    input_grad = unblocked(back_blocks).astype(jnp.bfloat16)
    lag_cur = jnp.einsum("gcbi,gcbk->gik", mixed_own, input_cur, preferred_element_type=jnp.float32)
    lag_prev = jnp.einsum(
        "gcbi,gcbk->gik", mixed_own, input_prev, preferred_element_type=jnp.float32
    )
    square = filter_len * filter_len
    front_part = jnp.pad(
        jnp.where(lower_mask, lag_cur, 0.0).reshape(groups_all, square), ((0, 0), (filter_len, 0))
    )
    rear_part = jnp.pad(
        jnp.where(lower_mask, 0.0, lag_prev).reshape(groups_all, square), ((0, 0), (0, filter_len))
    )
    skewed = (front_part + rear_part).reshape(groups_all, filter_len, filter_len + 1).sum(axis=1)
    local_grad = skewed[:, 1:][:, ::-1]
    grad_full = lax.psum(local_grad.astype(jnp.bfloat16), "zero").astype(jnp.float32)
    total_sq = jnp.sum(grad_full * grad_full)
    grad_shard = lax.dynamic_slice_in_dim(
        grad_full, lax.axis_index("zero") * shard_len, shard_len, 0
    )
    clip_scale = jnp.minimum(1.0, CLIP_NORM / (jnp.sqrt(total_sq) + 1e-06))
    clipped = grad_shard * clip_scale
    step_count = step_index[0].astype(jnp.float32) + 1.0
    moment_one = BETA_ONE * first_moment[0] + (1.0 - BETA_ONE) * clipped
    moment_two = BETA_TWO * second_moment[0] + (1.0 - BETA_TWO) * clipped * clipped
    corrected_one = moment_one / (1.0 - jnp.power(BETA_ONE, step_count))
    corrected_two = moment_two / (1.0 - jnp.power(BETA_TWO, step_count))
    stepped = filters[0] - LEARN_RATE * corrected_one / (jnp.sqrt(corrected_two) + ADAM_EPS)
    bit_count = lax.axis_size("rep").bit_length() - 1
    partner_bit = step_index[0] % bit_count
    branches = [partial(swap_bit, bit_number=number) for number in range(bit_count)]
    partner_values = lax.switch(partner_bit, branches, stepped)
    new_filters = 0.5 * (stepped + partner_values)
    return (query_grad[None], input_grad[None], new_filters[None])


def solution(mesh):
    return jax.shard_map(
        on_device,
        mesh=mesh,
        in_specs=(
            P("rep", "zero", None),
            P("rep", "zero", None),
            P("rep", "zero", None),
            P("rep", "zero", None),
            P("rep", "zero", None),
            P("rep", "zero", None),
            P(),
        ),
        out_specs=(P("rep", "zero", None), P("rep", "zero", None), P("rep", "zero", None)),
        check_vma=False,
    )
```

profile of v0, /device:TPU:8, one launch (start us, length us, event | category | flops | bytes accessed | tf_op | source)
XLA Modules:
  0.0 408.8 jit_solution(13536019468429333070)
XLA Ops:
  7.2 0.0 all-reduce.4.cloned.1.call-start
  7.2 1.9 collective-permute-start
  9.1 0.7 bitcast_convert_fusion
  9.8 23.5 %all_gather.3 = bf16[256,128]{1,0:T(8,128)(2,1)S(1)} all-gather(bf16[16,128]{1,0:T(8,128)(2,1)S(1)} %bitcast_convert_fusion), channel_id=1, replica_groups=mesh['rep'=2,'zero'=16] {'zero'}, dimensions={0}, use_global_device_ids=true | all-gather | bytes 69632 | tf_op jit(solution)/shard_map/all_gather | solution.py:58
  33.3 0.2 rev.6
  33.5 1.3 tile.4
  34.8 41.7 %copy.70 = bf16[32,8,128,256]{3,1,2,0:T(8,128)(2,1)S(1)} copy(bf16[32,8,128,256]{3,2,1,0:T(8,128)(2,1)S(1)} %bitcast.64) | data formatting | bytes 33554432
  76.5 6.6 %slice.29 = bf16[256,32640]{1,0:T(8,128)(2,1)} slice(bf16[256,32768]{1,0:T(8,128)(2,1)S(1)} %bitcast.65), slice={[0:256], [0:32640]} | slice | bytes 33423360 | tf_op jit(solution)/shard_map/slice | solution.py:31
  83.1 0.0 copy-start.6
  83.1 56.8 %reshape.85 = bf16[256,128,255]{2,1,0:T(8,128)(2,1)} reshape(bf16[256,32640]{1,0:T(8,128)(2,1)} %slice.29) | data formatting | bytes 33423360 | tf_op jit(solution)/shard_map/reshape | solution.py:32
  140.0 0.0 collective-permute-done
  140.0 0.0 copy-done.6
  140.0 1.4 maximum_bitcast_fusion
  141.4 2.5 copy.52
  143.9 2.5 reshape.83
  146.4 3.0 fusion.25
  149.4 0.0 copy-start.2
  149.4 0.0 copy-start.4
  149.4 9.6 %fusion.1 = f32[256,16,128]{2,1,0:T(8,128)S(1)} fusion(pred[128,128]{1,0:T(8,128)(4,1)S(1)} %iota_compare_fusion, bf16[256,128,255]{2,1,0:T(8,128)(2,1)} %reshape.85, bf16[256,16,1,128]{3,2,1,0:T(2,128)(2,1)S(1)} %get-tuple-element.12), kind=kOutput, calls=%fused_computation.6 | convolution fusion | flops 138412032 | bytes 11550720 | tf_op jit(solution)/shard_map/gik,gcbk->gcbi/dot_general | solution.py:79
  159.1 0.0 copy-done.2
  159.1 0.0 copy-done.4
  159.1 11.7 %fusion.10 = f32[256,16,128]{2,1,0:T(8,128)} fusion(f32[256,16,128]{2,1,0:T(8,128)S(1)} %fusion.1, pred[128,128]{1,0:T(8,128)(4,1)S(1)} %iota_compare_fusion, bf16[256,128,255]{2,1,0:T(8,128)(2,1)} %reshape.85, bf16[256,16,1,128]{3,2,1,0:T(2,128)(2,1)S(1)} %get-tuple-element.11), kind=kOutput, calls=%fused_computation.20 | convolution fusion | flops 138936320 | bytes 13647872 | tf_op jit(solution)/shard_map/gik,gcbk->gcbi/dot_general | solution.py:82
  170.8 2.1 copy.55
  172.9 3.0 fusion.9
  175.9 3.7 collective-permute-start.1
  180.3 11.6 %collective-permute-done.1 = bf16[128,4096]{1,0:T(8,128)(2,1)} collective-permute-done((bf16[128,4096]{1,0:T(8,128)(2,1)S(1)}, bf16[128,4096]{1,0:T(8,128)(2,1)}, u32[]{:S(2)}, u32[]{:S(2)}) %collective-permute-start.1) | collective-permute-done | bytes 1048608 | tf_op jit(solution)/shard_map/ppermute | solution.py:23
  191.9 1.4 maximum_bitcast_fusion.1
  193.3 2.5 copy.56
  195.8 2.5 reshape.88
  198.3 0.0 copy-start.5
  198.3 3.8 fusion.24
  202.1 0.0 copy-start
  202.1 0.0 copy-done.5
  202.1 0.0 copy-start.3
  202.1 7.2 %convolution_select_fusion = f32[256,128,128]{2,1,0:T(8,128)} fusion(pred[128,128]{1,0:T(8,128)(4,1)S(1)} %iota_compare_fusion, bf16[256,16,1,128]{3,2,1,0:T(2,128)(2,1)S(1)} %copy-done.5, bf16[256,16,1,128]{3,2,1,0:T(2,128)(2,1)S(1)} %get-tuple-element.10), kind=kOutput, calls=%fused_computation.1 | convolution fusion | flops 138412032 | bytes 18890752 | tf_op jit(solution)/shard_map/gcbi,gcbk->gik/dot_general | solution.py:94
  209.3 0.0 copy-done
  209.3 0.0 copy-done.3
  209.3 7.1 %convolution_select_fusion.1 = f32[256,128,128]{2,1,0:T(8,128)} fusion(pred[128,128]{1,0:T(8,128)(4,1)S(1)} %iota_compare_fusion, bf16[256,16,1,128]{3,2,1,0:T(2,128)(2,1)S(1)} %copy-done.3, bf16[256,16,1,128]{3,2,1,0:T(2,128)(2,1)S(1)} %get-tuple-element.10), kind=kOutput, calls=%fused_computation.2 | convolution fusion | flops 138412032 | bytes 18890752 | tf_op jit(solution)/shard_map/gcbi,gcbk->gik/dot_general | solution.py:93
  216.4 17.7 %copy.64 = f32[256,128,128]{0,2,1:T(8,128)} copy(f32[256,128,128]{2,1,0:T(8,128)} %convolution_select_fusion) | data formatting | bytes 33554432 | tf_op jit(solution)/shard_map/reshape | solution.py:102
  234.1 17.7 %copy.63 = f32[256,128,128]{0,2,1:T(8,128)} copy(f32[256,128,128]{2,1,0:T(8,128)} %convolution_select_fusion.1) | data formatting | bytes 33554432 | tf_op jit(solution)/shard_map/reshape | solution.py:99
  251.9 18.0 %pad_add_fusion = f32[256,16512]{0,1:T(8,128)} fusion(f32[256,16384]{0,1:T(8,128)} %bitcast.62, f32[256,16384]{0,1:T(8,128)} %bitcast.63), kind=kLoop, calls=%fused_computation | loop fusion | flops 4227072 | bytes 50462720 | tf_op jit(solution)/shard_map/add | solution.py:104
  269.9 18.0 %reshape.93 = f32[256,128,129]{0,2,1:T(8,128)} reshape(f32[256,16512]{0,1:T(8,128)} %pad_add_fusion) | data formatting | bytes 33816576 | tf_op jit(solution)/shard_map/reshape | solution.py:104
  287.9 0.0 copy-start.1
  287.9 7.3 %reduce_sum.18 = bf16[256,129]{0,1:T(8,128)(2,1)S(1)} reduce(f32[256,128,129]{0,2,1:T(8,128)} %reshape.93, f32[]{:T(128)} %constant.9.clone.1), dimensions={1}, to_apply=%region_0.1 | reduce | flops 4194048 | bytes 16974340 | tf_op jit(solution)/shard_map/reduce_sum | solution.py:104
  295.2 0.1 copy.69
  295.3 0.8 rev.7
  296.1 0.0 all-reduce.4.cloned.1.call-update
  296.1 0.0 copy-done.1
  296.1 0.0 copy-start.7
  296.2 0.0 copy-start.8
  296.2 0.0 copy-start.9
  296.2 10.4 %fusion = f32[256,16,128]{2,1,0:T(8,128)} fusion(pred[128,128]{1,0:T(8,128)(4,1)S(1)} %iota_compare_fusion, bf16[256,128,255]{2,1,0:T(8,128)(2,1)} %reshape.85, bf16[256,16,1,128]{3,2,1,0:T(2,128)(2,1)S(1)} %copy-done.1), kind=kOutput, calls=%fused_computation.5 | convolution fusion | flops 138412032 | bytes 11550720 | tf_op jit(solution)/shard_map/gki,gcbk->gcbi/dot_general | solution.py:86
  306.5 78.4 %all-reduce.4.cloned.1.call-done = bf16[256,128]{1,0:T(8,128)(2,1)} async-done(((bf16[256,128]{1,0:T(8,128)(2,1)}), bf16[256,128]{1,0:T(8,128)(2,1)}) %all-reduce.4.cloned.1.call-update) | async-done | bytes 65552 | tf_op jit(solution)/shard_map/psum | solution.py:106
  385.0 1.5 multiply_reduce_fusion
  387.2 0.9 convert_element_type.55
  388.0 0.0 copy-done.7
  388.0 0.0 copy-done.8
  388.1 0.0 copy-done.9
  388.1 1.5 collective-permute-start.2
  389.6 10.4 %add_convert_fusion = bf16[256,16,128]{2,1,0:T(8,128)(2,1)S(1)} fusion(f32[256,16,128]{2,1,0:T(8,128)} %fusion, pred[128,128]{1,0:T(8,128)(4,1)S(1)} %iota_compare_fusion, bf16[256,128,255]{2,1,0:T(8,128)(2,1)} %reshape.85, bf16[256,16,1,128]{3,2,1,0:T(2,128)(2,1)} %get-tuple-element.9), kind=kOutput, calls=%fused_computation.19 | convolution fusion | flops 139460608 | bytes 13647872 | tf_op jit(solution)/shard_map/gki,gcbk->gcbi/dot_general | solution.py:89
  400.0 1.3 copy.59
  401.3 0.0 collective-permute-done.2
  401.3 0.6 multiply_bitcast_fusion
  (4 shorter events, 0.1 us)
Async XLA Ops:
  7.2 377.8 %all-reduce.4.cloned.1.call-start = ((), (), s32[]{:S(2)}) async-start(), calls=%async_computation | async-start | bytes 131072 | tf_op jit(solution)/shard_map/psum | solution.py:106
  7.2 132.8 %collective-permute-start = (bf16[128,4096]{1,0:T(8,128)(2,1)}, bf16[128,4096]{1,0:T(8,128)(2,1)}, u32[]{:S(2)}, u32[]{:S(2)}) collective-permute-start(bf16[128,4096]{1,0:T(8,128)(2,1)} %bitcast.69), channel_id=1, source_target_pairs={{0,1},{1,2},{2,3},{3,4},{4,5},{5,6},{6,7},{7,8},{8,9},{9,10},{10,1... | collective-permute-start | bytes 3145736 | tf_op jit(solution)/shard_map/ppermute | solution.py:23
  83.1 56.8 %copy-start.6 = (bf16[1,128,4096]{2,1,0:T(8,128)(2,1)S(1)}, bf16[1,128,4096]{2,1,0:T(8,128)(2,1)}, u32[]{:S(2)}) copy-start(bf16[1,128,4096]{2,1,0:T(8,128)(2,1)} %param.7) | copy-start | bytes 3145732
  149.4 9.7 %copy-start.2 = (bf16[256,16,1,128]{3,2,1,0:T(2,128)(2,1)}, bf16[256,16,1,128]{3,2,1,0:T(2,128)(2,1)S(1)}, u32[]{:S(2)}) copy-start(bf16[256,16,1,128]{3,2,1,0:T(2,128)(2,1)S(1)} %get-tuple-element.12) | copy-start | bytes 3145732
  149.4 9.7 %copy-start.4 = (bf16[256,16,1,128]{3,2,1,0:T(2,128)(2,1)}, bf16[256,16,1,128]{3,2,1,0:T(2,128)(2,1)S(1)}, u32[]{:S(2)}) copy-start(bf16[256,16,1,128]{3,2,1,0:T(2,128)(2,1)S(1)} %get-tuple-element.11) | copy-start | bytes 3145732
  175.9 16.0 %collective-permute-start.1 = (bf16[128,4096]{1,0:T(8,128)(2,1)S(1)}, bf16[128,4096]{1,0:T(8,128)(2,1)}, u32[]{:S(2)}, u32[]{:S(2)}) collective-permute-start(bf16[128,4096]{1,0:T(8,128)(2,1)S(1)} %get-tuple-element.13), channel_id=1, source_target_pairs={{1,0},{2,1},{3,2},{4,3},{5,4},{6,5},{7,6},{8,7},{9,8},{10,9},{11,1... | collective-permute-start | bytes 3145736 | tf_op jit(solution)/shard_map/ppermute | solution.py:23
  198.3 3.8 copy-start.5
  202.1 7.2 %copy-start = (bf16[256,16,1,128]{3,2,1,0:T(2,128)(2,1)}, bf16[256,16,1,128]{3,2,1,0:T(2,128)(2,1)S(1)}, u32[]{:S(2)}) copy-start(bf16[256,16,1,128]{3,2,1,0:T(2,128)(2,1)S(1)} %get-tuple-element.10) | copy-start | bytes 3145732
  202.1 7.2 %copy-start.3 = (bf16[256,16,1,128]{3,2,1,0:T(2,128)(2,1)S(1)}, bf16[256,16,1,128]{3,2,1,0:T(2,128)(2,1)}, u32[]{:S(2)}) copy-start(bf16[256,16,1,128]{3,2,1,0:T(2,128)(2,1)} %copy-done.2) | copy-start | bytes 3145732
  287.9 8.3 %copy-start.1 = (bf16[256,16,1,128]{3,2,1,0:T(2,128)(2,1)S(1)}, bf16[256,16,1,128]{3,2,1,0:T(2,128)(2,1)}, u32[]{:S(2)}) copy-start(bf16[256,16,1,128]{3,2,1,0:T(2,128)(2,1)} %copy-done) | copy-start | bytes 3145732
  296.1 91.9 %copy-start.7 = (f32[1,16,128]{2,1,0:T(8,128)S(1)}, f32[1,16,128]{2,1,0:T(8,128)}, u32[]{:S(2)}) copy-start(f32[1,16,128]{2,1,0:T(8,128)} %param.10) | copy-start | bytes 24580
  296.2 91.9 %copy-start.8 = (f32[1,16,128]{2,1,0:T(8,128)S(1)}, f32[1,16,128]{2,1,0:T(8,128)}, u32[]{:S(2)}) copy-start(f32[1,16,128]{2,1,0:T(8,128)} %param.12) | copy-start | bytes 24580
  296.2 91.9 %copy-start.9 = (f32[1,16,128]{2,1,0:T(8,128)S(1)}, f32[1,16,128]{2,1,0:T(8,128)}, u32[]{:S(2)}) copy-start(f32[1,16,128]{2,1,0:T(8,128)} %param.11) | copy-start | bytes 24580
  388.1 13.2 %collective-permute-start.2 = (f32[16,128]{1,0:T(8,128)S(1)}, f32[16,128]{1,0:T(8,128)S(1)}, u32[]{:S(2)}, u32[]{:S(2)}) collective-permute-start(f32[16,128]{1,0:T(8,128)S(1)} %fusion.17), channel_id=1, source_target_pairs={{0,16},{16,0},{1,17},{17,1},{2,18},{18,2},{3,19},{19,3},{4,20},{20... | collective-permute-start | bytes 24584 | tf_op jit(solution)/shard_map/ppermute | solution.py:17
Sparse Core Ops, SparseCore 0:
  296.3 88.6 all-reduce.3
where the time goes:
time: 410 us; the launch traced here: 409 us
  local copies, waits for them, and re-layouts  181 us (44%)
  waiting for transfers between devices  90 us (22%)
  matrix products  56.3 us (14%)
  other arithmetic  34.8 us (8%)
  blocking collectives  23.5 us (6%)
  between operations  15.7 us (4%)
  starting transfers between devices  7.19 us (2%)
    psum x1, waiting for transfers between devices, on_device(): lax.psum(local_grad.astype(jnp.bfloat16), 'zero').astype(jnp.float32)  78.4 us
    reshape x1, local copies, waits for them, and re-layouts, circulant(): trimmed.reshape(groups_all, filter_len, 2 * filter_len - 1)  56.8 us
    unnamed x22, local copies, waits for them, and re-layouts  41.9 us
    all_gather x1, blocking collectives, on_device(): lax.all_gather(filters[0].astype(jnp.bfloat16), 'zero', axis=0, tiled=True)  23.5 us
    add x1, other arithmetic, on_device(): front_part + rear_part  18 us
    reshape x1, local copies, waits for them, and re-layouts, on_device(): (front_part + rear_part).reshape(groups_all, filter_len, filter_len + 1)  18 us
    reshape x1, local copies, waits for them, and re-layouts, on_device(): jnp.where(lower_mask, 0.0, lag_prev).reshape(groups_all, square)  17.7 us
    reshape x1, local copies, waits for them, and re-layouts, on_device(): jnp.where(lower_mask, lag_cur, 0.0).reshape(groups_all, square)  17.7 us
  transfers between devices with their start and end apart: 4, of which 2 were waited for; matrix products, arithmetic and copies ran while one was open for 32% of the time, Pallas kernels for 0%

commit v1 on v0

--- a/solution.py
+++ b/solution.py
@@ -55,7 +55,16 @@
     tok_rows, channels = inputs.shape
     filter_len = filters.shape[2]
     shard_len = filters.shape[1]
-    half_filters = lax.all_gather(filters[0].astype(jnp.bfloat16), "zero", axis=0, tiled=True)
+    sample = filters[0].astype(jnp.bfloat16)
+    half_filters = jnp.concatenate(
+        jax.lax.all_to_all(
+            jnp.stack([sample for _ in range(jax.lax.axis_size("zero"))]),
+            axis_name="zero",
+            split_axis=0,
+            concat_axis=0,
+        ),
+        axis=0,
+    )
     groups_all = half_filters.shape[0]
     circ_table = circulant(half_filters)
     index_row = lax.broadcasted_iota(jnp.int32, (filter_len, filter_len), 0)

time: 410 us -> 403 us (0.983)
  blocking collectives: 23.5 us -> 0 us
  waiting for transfers between devices: 90 us -> 100 us
  starting transfers between devices: 7.19 us -> 12 us
    all_gather x1 -> x0, blocking collectives: 23.5 us -> none  [on_device(): lax.all_gather(filters[0].astype(jnp.bfloat16), 'zero', axis=0, tiled=True)]
    all_to_all x0 -> x1, waiting for transfers between devices: none -> 8.32 us  [on_device(): jax.lax.all_to_all(jnp.stack([sample for _ in range(jax.lax.axis_size('ze...]
    all_to_all x0 -> x1, starting transfers between devices: none -> 6.57 us  [on_device(): jax.lax.all_to_all(jnp.stack([sample for _ in range(jax.lax.axis_size('ze...]
  transfers between devices with their start and end apart: 4 -> 5, of which waited for: 2 -> 3; matrix products, arithmetic and copies ran while one was open for 32% -> 32% of each run, Pallas kernels for 0% -> 0%
where the time goes in v1:
time: 403 us; the launch traced here: 401 us
  local copies, waits for them, and re-layouts  182 us (45%)
  waiting for transfers between devices  100 us (25%)
  matrix products  56.3 us (14%)
  other arithmetic  34.8 us (9%)
  between operations  15.7 us (4%)
  starting transfers between devices  12 us (3%)
    psum x1, waiting for transfers between devices, on_device(): lax.psum(local_grad.astype(jnp.bfloat16), 'zero').astype(jnp.float32)  80.4 us
    reshape x1, local copies, waits for them, and re-layouts, circulant(): trimmed.reshape(groups_all, filter_len, 2 * filter_len - 1)  56.8 us
    unnamed x22, local copies, waits for them, and re-layouts  41.9 us
    reshape x1, local copies, waits for them, and re-layouts, on_device(): (front_part + rear_part).reshape(groups_all, filter_len, filter_len + 1)  18 us
    add x1, other arithmetic, on_device(): front_part + rear_part  18 us
    reshape x1, local copies, waits for them, and re-layouts, on_device(): jnp.where(lower_mask, 0.0, lag_prev).reshape(groups_all, square)  17.8 us
    reshape x1, local copies, waits for them, and re-layouts, on_device(): jnp.where(lower_mask, lag_cur, 0.0).reshape(groups_all, square)  17.7 us
    dot_general x1, matrix products, on_device(): jnp.einsum('gik,gcbk->gcbi', table_prev, input_prev, preferred_element_ty...  11.7 us
  transfers between devices with their start and end apart: 5, of which 3 were waited for; matrix products, arithmetic and copies ran while one was open for 32% of the time, Pallas kernels for 0%

profile of v1, /device:TPU:8, one launch (start us, length us, event | category | flops | bytes accessed | tf_op | source)
XLA Modules:
  0.0 401.0 jit_solution(17119948520503934421)
XLA Ops:
  7.2 1.9 collective-permute-start
  9.1 0.7 convert_bitcast_fusion
  9.8 0.6 stack.5
  10.4 6.6 %all-to-all-start = ((bf16[16,16,128]{2,1,0:T(8,128)(2,1)}), bf16[16,16,128]{2,1,0:T(8,128)(2,1)S(1)}, u32[]{:S(2)}, u32[]{:S(2)}) async-start(bf16[16,16,128]{2,1,0:T(8,128)(2,1)} %stack.5), calls=%async_computation | async-start | bytes 131072 | tf_op jit(solution)/shard_map/all_to_all | solution.py:60
  17.0 0.0 all-reduce.4.cloned.1.call-start
  17.1 8.3 %all-to-all-done = bf16[16,16,128]{2,1,0:T(8,128)(2,1)S(1)} async-done(((bf16[16,16,128]{2,1,0:T(8,128)(2,1)}), bf16[16,16,128]{2,1,0:T(8,128)(2,1)S(1)}, u32[]{:S(2)}, u32[]{:S(2)}) %all-to-all-start) | async-done | bytes 65568 | tf_op jit(solution)/shard_map/all_to_all | solution.py:60
  25.4 0.2 rev.6
  25.6 1.3 tile.4
  26.9 41.7 %copy.54 = bf16[32,8,128,256]{3,1,2,0:T(8,128)(2,1)S(1)} copy(bf16[32,8,128,256]{3,2,1,0:T(8,128)(2,1)S(1)} %bitcast.66) | data formatting | bytes 33554432
  68.6 6.7 %slice.29 = bf16[256,32640]{1,0:T(8,128)(2,1)} slice(bf16[256,32768]{1,0:T(8,128)(2,1)S(1)} %bitcast.67), slice={[0:256], [0:32640]} | slice | bytes 33423360 | tf_op jit(solution)/shard_map/slice | solution.py:31
  75.3 0.0 copy-start.6
  75.3 56.8 %reshape.90 = bf16[256,128,255]{2,1,0:T(8,128)(2,1)} reshape(bf16[256,32640]{1,0:T(8,128)(2,1)} %slice.29) | data formatting | bytes 33423360 | tf_op jit(solution)/shard_map/reshape | solution.py:32
  132.1 0.0 collective-permute-done
  132.1 0.0 copy-done.6
  132.1 1.4 maximum_bitcast_fusion
  133.5 2.5 copy.36
  136.0 2.5 reshape.87
  138.5 3.0 fusion.25
  141.5 0.0 copy-start.2
  141.5 0.0 copy-start.4
  141.5 9.6 %fusion.1 = f32[256,16,128]{2,1,0:T(8,128)S(1)} fusion(pred[128,128]{1,0:T(8,128)(4,1)S(1)} %iota_compare_fusion, bf16[256,128,255]{2,1,0:T(8,128)(2,1)} %reshape.90, bf16[256,16,1,128]{3,2,1,0:T(2,128)(2,1)S(1)} %get-tuple-element.9), kind=kOutput, calls=%fused_computation.6 | convolution fusion | flops 138412032 | bytes 11550720 | tf_op jit(solution)/shard_map/gik,gcbk->gcbi/dot_general | solution.py:88
  151.2 0.0 copy-done.2
  151.2 0.0 copy-done.4
  151.2 11.7 %fusion.10 = f32[256,16,128]{2,1,0:T(8,128)} fusion(f32[256,16,128]{2,1,0:T(8,128)S(1)} %fusion.1, pred[128,128]{1,0:T(8,128)(4,1)S(1)} %iota_compare_fusion, bf16[256,128,255]{2,1,0:T(8,128)(2,1)} %reshape.90, bf16[256,16,1,128]{3,2,1,0:T(2,128)(2,1)S(1)} %get-tuple-element.8), kind=kOutput, calls=%fused_computation.20 | convolution fusion | flops 138936320 | bytes 13647872 | tf_op jit(solution)/shard_map/gik,gcbk->gcbi/dot_general | solution.py:91
  162.8 2.1 copy.39
  164.9 3.0 fusion.9
  168.0 1.9 collective-permute-start.1
  170.6 11.6 %collective-permute-done.1 = bf16[128,4096]{1,0:T(8,128)(2,1)} collective-permute-done((bf16[128,4096]{1,0:T(8,128)(2,1)S(1)}, bf16[128,4096]{1,0:T(8,128)(2,1)}, u32[]{:S(2)}, u32[]{:S(2)}) %collective-permute-start.1) | collective-permute-done | bytes 1048608 | tf_op jit(solution)/shard_map/ppermute | solution.py:23
  182.2 1.4 maximum_bitcast_fusion.1
  183.6 2.5 copy.40
  186.0 2.5 reshape.93
  188.6 0.0 copy-start.5
  188.6 3.8 fusion.24
  192.4 0.0 copy-start
  192.4 0.0 copy-done.5
  192.4 0.0 copy-start.3
  192.4 7.2 %convolution_select_fusion = f32[256,128,128]{2,1,0:T(8,128)} fusion(pred[128,128]{1,0:T(8,128)(4,1)S(1)} %iota_compare_fusion, bf16[256,16,1,128]{3,2,1,0:T(2,128)(2,1)S(1)} %copy-done.5, bf16[256,16,1,128]{3,2,1,0:T(2,128)(2,1)S(1)} %get-tuple-element.7), kind=kOutput, calls=%fused_computation.1 | convolution fusion | flops 138412032 | bytes 18890752 | tf_op jit(solution)/shard_map/gcbi,gcbk->gik/dot_general | solution.py:103
  199.6 0.0 copy-done
  199.6 0.0 copy-done.3
  199.6 7.1 %convolution_select_fusion.1 = f32[256,128,128]{2,1,0:T(8,128)} fusion(pred[128,128]{1,0:T(8,128)(4,1)S(1)} %iota_compare_fusion, bf16[256,16,1,128]{3,2,1,0:T(2,128)(2,1)S(1)} %copy-done.3, bf16[256,16,1,128]{3,2,1,0:T(2,128)(2,1)S(1)} %get-tuple-element.7), kind=kOutput, calls=%fused_computation.2 | convolution fusion | flops 138412032 | bytes 18890752 | tf_op jit(solution)/shard_map/gcbi,gcbk->gik/dot_general | solution.py:102
  206.7 17.8 %copy.48 = f32[256,128,128]{0,2,1:T(8,128)} copy(f32[256,128,128]{2,1,0:T(8,128)} %convolution_select_fusion) | data formatting | bytes 33554432 | tf_op jit(solution)/shard_map/reshape | solution.py:111
  224.4 17.7 %copy.47 = f32[256,128,128]{0,2,1:T(8,128)} copy(f32[256,128,128]{2,1,0:T(8,128)} %convolution_select_fusion.1) | data formatting | bytes 33554432 | tf_op jit(solution)/shard_map/reshape | solution.py:108
  242.2 18.0 %pad_add_fusion = f32[256,16512]{0,1:T(8,128)} fusion(f32[256,16384]{0,1:T(8,128)} %bitcast.64, f32[256,16384]{0,1:T(8,128)} %bitcast.65), kind=kLoop, calls=%fused_computation | loop fusion | flops 4227072 | bytes 50462720 | tf_op jit(solution)/shard_map/add | solution.py:113
  260.2 18.0 %reshape.98 = f32[256,128,129]{0,2,1:T(8,128)} reshape(f32[256,16512]{0,1:T(8,128)} %pad_add_fusion) | data formatting | bytes 33816576 | tf_op jit(solution)/shard_map/reshape | solution.py:113
  278.2 7.3 %reduce_sum.18 = bf16[256,129]{0,1:T(8,128)(2,1)S(1)} reduce(f32[256,128,129]{0,2,1:T(8,128)} %reshape.98, f32[]{:T(128)} %constant.9.clone.1), dimensions={1}, to_apply=%region_0.1 | reduce | flops 4194048 | bytes 16974340 | tf_op jit(solution)/shard_map/reduce_sum | solution.py:113
  285.5 0.1 copy.53
  285.6 0.8 rev.7
  286.4 0.0 all-reduce.4.cloned.1.call-update
  286.4 0.0 copy-done.1
  286.5 0.0 copy-start.7
  286.5 0.0 copy-start.8
  286.5 0.0 copy-start.9
  286.5 10.3 %fusion = f32[256,16,128]{2,1,0:T(8,128)} fusion(pred[128,128]{1,0:T(8,128)(4,1)S(1)} %iota_compare_fusion, bf16[256,128,255]{2,1,0:T(8,128)(2,1)} %reshape.90, bf16[256,16,1,128]{3,2,1,0:T(2,128)(2,1)S(1)} %copy-done.1), kind=kOutput, calls=%fused_computation.5 | convolution fusion | flops 138412032 | bytes 11550720 | tf_op jit(solution)/shard_map/gki,gcbk->gcbi/dot_general | solution.py:95
  296.8 80.4 %all-reduce.4.cloned.1.call-done = bf16[256,128]{1,0:T(8,128)(2,1)} async-done(((bf16[256,128]{1,0:T(8,128)(2,1)}), bf16[256,128]{1,0:T(8,128)(2,1)}) %all-reduce.4.cloned.1.call-update) | async-done | bytes 65552 | tf_op jit(solution)/shard_map/psum | solution.py:115
  377.2 1.5 multiply_reduce_fusion
  379.4 0.9 convert_element_type.56
  380.3 0.0 copy-done.7
  380.3 0.0 copy-done.8
  380.3 0.0 copy-done.9
  380.3 1.5 collective-permute-start.2
  381.9 10.4 %add_convert_fusion = bf16[256,16,128]{2,1,0:T(8,128)(2,1)S(1)} fusion(f32[256,16,128]{2,1,0:T(8,128)} %fusion, pred[128,128]{1,0:T(8,128)(4,1)S(1)} %iota_compare_fusion, bf16[256,128,255]{2,1,0:T(8,128)(2,1)} %reshape.90, bf16[256,16,1,128]{3,2,1,0:T(2,128)(2,1)} %get-tuple-element.6), kind=kOutput, calls=%fused_computation.19 | convolution fusion | flops 139460608 | bytes 13647872 | tf_op jit(solution)/shard_map/gki,gcbk->gcbi/dot_general | solution.py:98
  392.2 1.3 copy.43
  393.6 0.0 collective-permute-done.2
  393.6 0.6 multiply_bitcast_fusion
  (5 shorter events, 0.1 us)
Async XLA Ops:
  7.2 124.9 %collective-permute-start = (bf16[128,4096]{1,0:T(8,128)(2,1)}, bf16[128,4096]{1,0:T(8,128)(2,1)}, u32[]{:S(2)}, u32[]{:S(2)}) collective-permute-start(bf16[128,4096]{1,0:T(8,128)(2,1)} %bitcast.71), channel_id=1, source_target_pairs={{0,1},{1,2},{2,3},{3,4},{4,5},{5,6},{6,7},{7,8},{8,9},{9,10},{10,1... | collective-permute-start | bytes 3145736 | tf_op jit(solution)/shard_map/ppermute | solution.py:23
  10.4 15.0 %all-to-all-start = ((bf16[16,16,128]{2,1,0:T(8,128)(2,1)}), bf16[16,16,128]{2,1,0:T(8,128)(2,1)S(1)}, u32[]{:S(2)}, u32[]{:S(2)}) async-start(bf16[16,16,128]{2,1,0:T(8,128)(2,1)} %stack.5), calls=%async_computation | async-start | bytes 131072 | tf_op jit(solution)/shard_map/all_to_all | solution.py:60
  17.0 360.2 %all-reduce.4.cloned.1.call-start = ((), (), s32[]{:S(2)}) async-start(), calls=%async_computation.1 | async-start | bytes 131072 | tf_op jit(solution)/shard_map/psum | solution.py:115
  75.3 56.8 %copy-start.6 = (bf16[1,128,4096]{2,1,0:T(8,128)(2,1)S(1)}, bf16[1,128,4096]{2,1,0:T(8,128)(2,1)}, u32[]{:S(2)}) copy-start(bf16[1,128,4096]{2,1,0:T(8,128)(2,1)} %param.7) | copy-start | bytes 3145732
  141.5 9.7 %copy-start.2 = (bf16[256,16,1,128]{3,2,1,0:T(2,128)(2,1)}, bf16[256,16,1,128]{3,2,1,0:T(2,128)(2,1)S(1)}, u32[]{:S(2)}) copy-start(bf16[256,16,1,128]{3,2,1,0:T(2,128)(2,1)S(1)} %get-tuple-element.9) | copy-start | bytes 3145732
  141.5 9.7 %copy-start.4 = (bf16[256,16,1,128]{3,2,1,0:T(2,128)(2,1)}, bf16[256,16,1,128]{3,2,1,0:T(2,128)(2,1)S(1)}, u32[]{:S(2)}) copy-start(bf16[256,16,1,128]{3,2,1,0:T(2,128)(2,1)S(1)} %get-tuple-element.8) | copy-start | bytes 3145732
  168.0 14.2 %collective-permute-start.1 = (bf16[128,4096]{1,0:T(8,128)(2,1)S(1)}, bf16[128,4096]{1,0:T(8,128)(2,1)}, u32[]{:S(2)}, u32[]{:S(2)}) collective-permute-start(bf16[128,4096]{1,0:T(8,128)(2,1)S(1)} %get-tuple-element.10), channel_id=1, source_target_pairs={{1,0},{2,1},{3,2},{4,3},{5,4},{6,5},{7,6},{8,7},{9,8},{10,9},{11,1... | collective-permute-start | bytes 3145736 | tf_op jit(solution)/shard_map/ppermute | solution.py:23
  188.6 3.8 copy-start.5
  192.4 7.2 %copy-start = (bf16[256,16,1,128]{3,2,1,0:T(2,128)(2,1)}, bf16[256,16,1,128]{3,2,1,0:T(2,128)(2,1)S(1)}, u32[]{:S(2)}) copy-start(bf16[256,16,1,128]{3,2,1,0:T(2,128)(2,1)S(1)} %get-tuple-element.7) | copy-start | bytes 3145732
  192.4 7.2 %copy-start.3 = (bf16[256,16,1,128]{3,2,1,0:T(2,128)(2,1)S(1)}, bf16[256,16,1,128]{3,2,1,0:T(2,128)(2,1)}, u32[]{:S(2)}) copy-start(bf16[256,16,1,128]{3,2,1,0:T(2,128)(2,1)} %copy-done.2) | copy-start | bytes 3145732
  278.2 8.3 %copy-start.1 = (bf16[256,16,1,128]{3,2,1,0:T(2,128)(2,1)S(1)}, bf16[256,16,1,128]{3,2,1,0:T(2,128)(2,1)}, u32[]{:S(2)}) copy-start(bf16[256,16,1,128]{3,2,1,0:T(2,128)(2,1)} %copy-done) | copy-start | bytes 3145732
  286.5 93.8 %copy-start.7 = (f32[1,16,128]{2,1,0:T(8,128)S(1)}, f32[1,16,128]{2,1,0:T(8,128)}, u32[]{:S(2)}) copy-start(f32[1,16,128]{2,1,0:T(8,128)} %param.10) | copy-start | bytes 24580
  286.5 93.8 %copy-start.8 = (f32[1,16,128]{2,1,0:T(8,128)S(1)}, f32[1,16,128]{2,1,0:T(8,128)}, u32[]{:S(2)}) copy-start(f32[1,16,128]{2,1,0:T(8,128)} %param.12) | copy-start | bytes 24580
  286.5 93.8 %copy-start.9 = (f32[1,16,128]{2,1,0:T(8,128)S(1)}, f32[1,16,128]{2,1,0:T(8,128)}, u32[]{:S(2)}) copy-start(f32[1,16,128]{2,1,0:T(8,128)} %param.11) | copy-start | bytes 24580
  380.3 13.2 %collective-permute-start.2 = (f32[16,128]{1,0:T(8,128)S(1)}, f32[16,128]{1,0:T(8,128)S(1)}, u32[]{:S(2)}, u32[]{:S(2)}) collective-permute-start(f32[16,128]{1,0:T(8,128)S(1)} %fusion.17), channel_id=1, source_target_pairs={{0,16},{16,0},{1,17},{17,1},{2,18},{18,2},{3,19},{19,3},{4,20},{20... | collective-permute-start | bytes 24584 | tf_op jit(solution)/shard_map/ppermute | solution.py:17
Sparse Core Ops, SparseCore 0:
  286.6 90.6 all-reduce.3
